TPU v7x, 32 devices: a whole 2x2x4 slice. The times are simulated.
32 devices in a mesh: cls: 4 (over x, core), prt: 8 (over z, y).
Axes of the slice: x: 2, y: 2, z: 4, core: 2. Of those that a mesh axis runs over, the one named last changes fastest.
Arguments:
- images: bfloat16 [4096, 7168], P(('cls', 'prt')), may hold values from -48 to 48
- projections: bfloat16 [8, 144, 7168], P('cls', None, 'prt'), may hold values from -5 to 5
- noise_weights: float32 [7168], replicated, may hold values from 0.005 to 0.03
- class_prior: float32 [8], replicated, may hold values from 0.05 to 1
- class_lists: int32 [4096, 2], P(('cls', 'prt')), may hold values from 0 to 7, all different within a row; in each aligned block of 128 rows (0 to 127, 128 to 255, ...) at most 40 rows name the same one
Outputs:
- class_sums: float32 [8, 144, 7168], P('cls', None, 'prt')
- class_weights: float32 [8, 144], P('cls')
- evidence: float32 [4096], P(('cls', 'prt'))
Inputs may be any that keep to these rules, and one draw needn't show every extreme that they name: `class_lists`: each row names 2 different classes; in the rows of one device no class is named by more than 40 rows, a bound that some block reaches.
All inputs are finite; a program needn't handle non-finite values.
Results may differ from a plain program's by a relative error of at most 0.0066.
Values may be sent and summed in bfloat16 or wider, within the bound.
No kernel may reach another device: no remote copies, remote signals or barrier semaphores. Data moves between devices by JAX's collectives and lax.ppermute only.
A program may use at most 128 MiB of HBM per device.

v0:
```python
import jax
import jax.numpy as jnp
from jax import lax
from jax.sharding import PartitionSpec as P


def score_columns(slab, weighted, noise_weights):
    count = slab.shape[0]
    orient = slab.shape[1]
    nrows = weighted.shape[0]
    piece = lax.all_gather(slab, "prt", axis=2, tiled=True)
    span = piece.shape[2]
    flat = piece.reshape(count * orient, span)
    cross = lax.dot_general(
        weighted, flat, (((1,), (1,)), ((), ())), preferred_element_type=jnp.float32
    )
    square = piece.astype(jnp.float32)
    norms = 0.5 * jnp.sum(square * square * noise_weights[None, None, :], axis=2).reshape(
        count * orient
    )
    cross, norms = (cross, norms)
    return (cross - norms[None, :]).reshape(nrows, count, orient)


def posterior(score, log_prior, listed):
    score = score + log_prior[None, :, None]
    score = jnp.where(listed[:, :, None], score, -jnp.inf)
    top = jnp.max(score, axis=(1, 2))
    total = jnp.sum(jnp.exp(score - top[:, None, None]), axis=(1, 2))
    evid = top + jnp.log(total)
    post = jnp.exp(score - evid[:, None, None]).astype(jnp.bfloat16)
    return (evid, post)


def local(images, projections, noise_weights, class_prior, class_lists):
    groups = lax.axis_size("cls")
    owned = projections.shape[0]
    classes = owned * groups
    log_prior = jnp.log(class_prior)
    listed = jnp.any(
        class_lists[:, :, None] == jnp.arange(classes, dtype=jnp.int32)[None, None, :], axis=1
    )
    everyone = lax.all_gather(images, "cls", axis=0, tiled=True)
    weighted = (everyone.astype(jnp.float32) * noise_weights[None, :]).astype(jnp.bfloat16)
    own_scores = score_columns(projections, weighted, noise_weights)
    score = lax.all_to_all(own_scores, "cls", split_axis=0, concat_axis=1, tiled=True)
    evidence, post = posterior(score, log_prior, listed)
    mine = lax.all_to_all(post, "cls", split_axis=1, concat_axis=0, tiled=True)
    sums = jnp.einsum("ijr,if->jrf", mine, everyone, preferred_element_type=jnp.float32)
    totals = jnp.sum(mine.astype(jnp.float32), axis=0)
    class_sums = lax.psum_scatter(sums, "prt", scatter_dimension=2, tiled=True)
    class_weights = lax.psum(totals, "prt")
    return (class_sums, class_weights, evidence)


def solution(mesh):
    return jax.shard_map(
        local,
        mesh=mesh,
        in_specs=(
            P(("cls", "prt"), None),
            P("cls", None, "prt"),
            P(),
            P(),
            P(("cls", "prt"), None),
        ),
        out_specs=(P("cls", None, "prt"), P("cls", None), P(("cls", "prt"))),
        check_vma=False,
    )
```

profile of v0, /device:TPU:0, one launch (start us, length us, event | category | flops | bytes accessed | tf_op | source)
XLA Modules:
  0.0 335.4 jit_solution(646722921677598677)
XLA Ops:
  7.2 0.0 all-gather.5.cloned.1.call-start
  7.2 0.7 all-gather.5.cloned.1.call-update
  7.9 0.0 all-gather.3.cloned.1.call-start
  7.9 0.7 all-gather.3.cloned.1.call-update
  8.6 76.2 %all-gather.5.cloned.1.call-done = bf16[2,144,7168]{2,1,0:T(8,128)(2,1)} async-done(((bf16[2,144,896]{2,1,0:T(8,128)(2,1)}), bf16[2,144,7168]{2,1,0:T(8,128)(2,1)}) %all-gather.5.cloned.1.call-update) | async-done | bytes 4128784 | tf_op jit(solution)/shard_map/all_gather | solution.py:11
  84.9 3.3 multiply_reduce_fusion
  88.2 0.1 mul.39
  88.3 49.0 %all-gather.3.cloned.1.call-done = bf16[512,7168]{1,0:T(8,128)(2,1)} async-done(((bf16[128,7168]{1,0:T(8,128)(2,1)}), bf16[512,7168]{1,0:T(8,128)(2,1)}) %all-gather.3.cloned.1.call-update) | async-done | bytes 7340048 | tf_op jit(solution)/shard_map/all_gather | solution.py:43
  137.3 0.0 copy-start
  137.3 0.0 copy-start.2
  137.3 6.6 %fusion.4 = f32[512,288]{0,1:T(8,128)S(1)} fusion(bf16[288,7168]{1,0:T(8,128)(2,1)} %bitcast.31, bf16[512,7168]{1,0:T(8,128)(2,1)} %all-gather.3.cloned.1.call-done, f32[7168]{0:T(1024)} %param.7, f32[288]{0:T(512)S(1)} %mul.39), kind=kOutput, calls=%fused_computation.6 | convolution fusion | flops 2125086720 | bytes 12088448 | tf_op jit(solution)/shard_map/dot_general | solution.py:14
  143.9 1.3 copy.24
  145.2 3.5 %all-to-all-start = ((f32[512,2,144]{2,1,0:T(2,128)}), f32[512,2,144]{2,1,0:T(2,128)S(1)}, u32[]{:S(2)}, u32[]{:S(2)}) async-start(f32[512,2,144]{2,1,0:T(2,128)} %copy.24), calls=%async_computation | async-start | bytes 2097152 | tf_op jit(solution)/shard_map/all_to_all | solution.py:46
  148.8 0.0 reduce-scatter.2.cloned.1.call-start
  148.8 0.0 copy-done
  148.9 0.0 copy-done.2
  148.9 0.1 add.29
  149.0 0.1 copy.28
  149.1 14.1 %all-to-all-done = f32[512,2,144]{2,1,0:T(2,128)S(1)} async-done(((f32[512,2,144]{2,1,0:T(2,128)}), f32[512,2,144]{2,1,0:T(2,128)S(1)}, u32[]{:S(2)}, u32[]{:S(2)}) %all-to-all-start) | async-done | bytes 589856 | tf_op jit(solution)/shard_map/all_to_all | solution.py:46
  163.2 1.0 copy.30
  164.2 0.4 fusion.9
  164.6 0.4 exponential_reduce_fusion
  165.0 0.0 copy-start.1
  165.0 0.2 fusion.8
  165.2 8.7 %all_to_all.36 = bf16[128,8,144]{0,2,1:T(8,128)(2,1)S(1)} all-to-all(bf16[128,8,144]{0,2,1:T(8,128)(2,1)S(1)} %fusion.8), channel_id=1, replica_groups=mesh['cls'=4,'prt'=8] {'cls'}, dimensions={1} | all-to-all | bytes 589824 | tf_op jit(solution)/shard_map/all_to_all | solution.py:48
  173.9 8.6 %fusion.1 = f32[2,144,7168]{2,1,0:T(8,128)} fusion(bf16[512,7168]{1,0:T(8,128)(2,1)} %all-gather.3.cloned.1.call-done, bf16[4,2,18,8,128]{4,3,2,1,0:T(8,128)(2,1)S(1)} %bitcast.32), kind=kOutput, calls=%fused_computation.3 | convolution fusion | flops 2113929216 | bytes 15892480 | tf_op jit(solution)/shard_map/ijr,if->jrf/dot_general | solution.py:49
  182.5 0.0 copy-done.1
  182.5 0.0 reduce-scatter.2.cloned.1.call-update
  182.5 0.2 convert_reduce_fusion
  182.7 22.6 %psum.7 = f32[2,144]{1,0:T(2,128)} all-reduce(f32[2,144]{1,0:T(2,128)S(1)} %convert_reduce_fusion), channel_id=1, replica_groups=mesh['cls'=4,'prt'=8] {'prt'}, use_global_device_ids=true, to_apply=%region_6.7 | all-reduce | flops 288 | bytes 2304 | tf_op jit(solution)/shard_map/psum | solution.py:52
  205.3 123.5 %reduce-scatter.2.cloned.1.call-done = f32[2,144,896]{2,1,0:T(8,128)} async-done(((f32[2,144,7168]{2,1,0:T(8,128)}), f32[2,144,896]{2,1,0:T(8,128)}) %reduce-scatter.2.cloned.1.call-update) | async-done | bytes 1032208 | tf_op jit(solution)/shard_map/reduce_scatter | solution.py:51
  (7 shorter events, 0.1 us)
Async XLA Ops:
  7.2 77.7 %all-gather.5.cloned.1.call-start = ((), (), s32[]{:S(2)}) async-start(), calls=%async_computation.4 | async-start | bytes 4644864 | tf_op jit(solution)/shard_map/all_gather | solution.py:11
  7.9 129.4 %all-gather.3.cloned.1.call-start = ((), (), s32[]{:S(2)}) async-start(), calls=%async_computation.3 | async-start | bytes 9175040 | tf_op jit(solution)/shard_map/all_gather | solution.py:43
  137.3 11.5 %copy-start = (s32[128,2]{0,1:T(2,128)S(1)}, s32[128,2]{0,1:T(2,128)}, u32[]{:S(2)}) copy-start(s32[128,2]{0,1:T(2,128)} %param.9) | copy-start | bytes 3076
  137.3 11.6 %copy-start.2 = (f32[8]{0:T(128)S(1)}, f32[8]{0:T(128)}, u32[]{:S(2)}) copy-start(f32[8]{0:T(128)} %param.8) | copy-start | bytes 100
  145.2 17.9 %all-to-all-start = ((f32[512,2,144]{2,1,0:T(2,128)}), f32[512,2,144]{2,1,0:T(2,128)S(1)}, u32[]{:S(2)}, u32[]{:S(2)}) async-start(f32[512,2,144]{2,1,0:T(2,128)} %copy.24), calls=%async_computation | async-start | bytes 2097152 | tf_op jit(solution)/shard_map/all_to_all | solution.py:46
  148.8 180.1 %reduce-scatter.2.cloned.1.call-start = ((), (), s32[]{:S(2)}) async-start(), calls=%async_computation.5 | async-start | bytes 9289728 | tf_op jit(solution)/shard_map/reduce_scatter | solution.py:51
  165.0 17.5 %copy-start.1 = (f32[128]{0:T(128)}, f32[128]{0:T(128)S(1)}, u32[]{:S(2)}) copy-start(f32[128]{0:T(128)S(1)} %log_add_fusion) | copy-start | bytes 1540
Sparse Core Ops, SparseCore 0:
  10.1 74.7 all-gather.4
  86.4 50.8 all-gather.2
  182.6 146.1 reduce-scatter.1
where the time goes:
time: 336 us; the launch traced here: 335 us
  waiting for transfers between devices  264 us (79%)
  blocking collectives  31.3 us (9%)
  matrix products  15.2 us (5%)
  between operations  13.8 us (4%)
  other arithmetic  4.49 us (1%)
  starting transfers between devices  3.63 us (1%)
    reduce_scatter x1, waiting for transfers between devices, local(): class_sums = lax.psum_scatter(sums, 'prt', scatter_dimension=2, tiled=True)  124 us
    all_gather x1, waiting for transfers between devices, score_columns(): piece = lax.all_gather(slab, 'prt', axis=2, tiled=True)  76.2 us
    all_gather x1, waiting for transfers between devices, local(): everyone = lax.all_gather(images, 'cls', axis=0, tiled=True)  49 us
    psum x1, blocking collectives, local(): class_weights = lax.psum(totals, 'prt')  22.6 us
    all_to_all x1, waiting for transfers between devices, local(): lax.all_to_all(own_scores, 'cls', split_axis=0, concat_axis=1, tiled=True)  14.1 us
    all_to_all x1, blocking collectives, local(): mine = lax.all_to_all(post, 'cls', split_axis=1, concat_axis=0, tiled=True)  8.72 us
    dot_general x1, matrix products, local(): jnp.einsum('ijr,if->jrf', mine, everyone, preferred_element_type=jnp.floa...  8.56 us
  transfers between devices with their start and end apart: 4, of which 4 were waited for; matrix products, arithmetic and copies ran while one was open for 1% of the time, Pallas kernels for 0%

commit v1 on v0

--- a/solution.py
+++ b/solution.py
@@ -4,11 +4,29 @@
 from jax.sharding import PartitionSpec as P
 
 
+def joined_along(blocks, dim):
+    blocks = jnp.moveaxis(blocks, 0, dim)
+    shape = blocks.shape
+    return blocks.reshape(*shape[:dim], shape[dim] * shape[dim + 1], *shape[dim + 2 :])
+
+
 def score_columns(slab, weighted, noise_weights):
     count = slab.shape[0]
     orient = slab.shape[1]
     nrows = weighted.shape[0]
-    piece = lax.all_gather(slab, "prt", axis=2, tiled=True)
+    size = lax.axis_size("prt")
+    pairs = [(i, (i + 1) % size) for i in range(size)]
+    back = [(b, a) for a, b in pairs]
+    lower, upper = ([], [])
+    for lap in range(size - 1):
+        if lap % 2 == 0:
+            lower.append(lax.ppermute(lower[-1] if lower else slab, "prt", pairs))
+        else:
+            upper.append(lax.ppermute(upper[-1] if upper else slab, "prt", back))
+    parts = jnp.stack([*lower[::-1], slab, *upper])
+    shift = lax.axis_index("prt") - len(lower)
+    parts = parts[(jnp.arange(size) - shift) % size]
+    piece = joined_along(parts, 2)
     span = piece.shape[2]
     flat = piece.reshape(count * orient, span)
     cross = lax.dot_general(

time: 336 us -> 313 us (0.932)
  waiting for transfers between devices: 264 us -> 187 us
  starting transfers between devices: 3.63 us -> 41.1 us
  local copies, waits for them, and re-layouts: 2.64 us -> 22.9 us
    all_gather x1 -> x0, waiting for transfers between devices: 76.2 us -> none  [score_columns(): piece = lax.all_gather(slab, 'prt', axis=2, tiled=True)]
    all_gather x1, waiting for transfers between devices: 49 us -> 0.01 us  [local(): everyone = lax.all_gather(images, 'cls', axis=0, tiled=True)]
    ppermute x0 -> x7, waiting for transfers between devices: none -> 48.7 us  [the longest x4 48.7 us: score_columns(): lower.append(lax.ppermute(lower[-1] if lower else slab, 'prt', pairs))]
    ppermute x0 -> x7, starting transfers between devices: none -> 37.5 us  [the longest x3 29.5 us: score_columns(): upper.append(lax.ppermute(upper[-1] if upper else slab, 'prt', back))]
    unnamed x6 -> x20, local copies, waits for them, and re-layouts: 0.01 us -> 10 us
    gather x0 -> x1, local copies, waits for them, and re-layouts: none -> 5.12 us  [score_columns(): parts = parts[(jnp.arange(size) - shift) % size]]
    transpose x0 -> x1, local copies, waits for them, and re-layouts: none -> 3.55 us  [joined_along(): blocks = jnp.moveaxis(blocks, 0, dim)]
  transfers between devices with their start and end apart: 4 -> 10, of which waited for: 4 -> 6; matrix products, arithmetic and copies ran while one was open for 1% -> 7% of each run, Pallas kernels for 0% -> 0%
where the time goes in v1:
time: 313 us; the launch traced here: 312 us
  waiting for transfers between devices  187 us (60%)
  starting transfers between devices  41.1 us (13%)
  blocking collectives  29.8 us (10%)
  local copies, waits for them, and re-layouts  22.9 us (7%)
  matrix products  15.2 us (5%)
  between operations  14.2 us (5%)
    reduce_scatter x1, waiting for transfers between devices, local(): class_sums = lax.psum_scatter(sums, 'prt', scatter_dimension=2, tiled=True)  123 us
    ppermute x4, waiting for transfers between devices, score_columns(): lower.append(lax.ppermute(lower[-1] if lower else slab, 'prt', pairs))  48.7 us
    ppermute x3, starting transfers between devices, score_columns(): upper.append(lax.ppermute(upper[-1] if upper else slab, 'prt', back))  29.5 us
    psum x1, blocking collectives, local(): class_weights = lax.psum(totals, 'prt')  21 us
    all_to_all x1, waiting for transfers between devices, local(): lax.all_to_all(own_scores, 'cls', split_axis=0, concat_axis=1, tiled=True)  14.1 us
    unnamed x20, local copies, waits for them, and re-layouts  10 us
    all_to_all x1, blocking collectives, local(): mine = lax.all_to_all(post, 'cls', split_axis=1, concat_axis=0, tiled=True)  8.72 us
    dot_general x1, matrix products, local(): jnp.einsum('ijr,if->jrf', mine, everyone, preferred_element_type=jnp.floa...  8.56 us
  transfers between devices with their start and end apart: 10, of which 6 were waited for; matrix products, arithmetic and copies ran while one was open for 7% of the time, Pallas kernels for 0%

profile of v1, /device:TPU:0, one launch (start us, length us, event | category | flops | bytes accessed | tf_op | source)
XLA Modules:
  0.0 312.2 jit_solution(13175010031791548189)
XLA Ops:
  7.2 0.0 all-gather.2.cloned.1.call-start
  7.2 0.7 all-gather.2.cloned.1.call-update
  7.9 3.0 collective-permute-start
  11.0 15.0 %collective-permute-done = bf16[2,144,896]{2,1,0:T(8,128)(2,1)S(1)} collective-permute-done((bf16[2,144,896]{2,1,0:T(8,128)(2,1)}, bf16[2,144,896]{2,1,0:T(8,128)(2,1)S(1)}, u32[]{:S(2)}, u32[]{:S(2)}) %collective-permute-start) | collective-permute-done | bytes 516128 | tf_op jit(solution)/shard_map/ppermute | solution.py:23
  26.0 0.0 collective-permute-start.1
  26.0 4.7 %collective-permute-start.4 = (bf16[2,144,896]{2,1,0:T(8,128)(2,1)}, bf16[2,144,896]{2,1,0:T(8,128)(2,1)S(1)}, u32[]{:S(2)}, u32[]{:S(2)}) collective-permute-start(bf16[2,144,896]{2,1,0:T(8,128)(2,1)} %param.6), channel_id=1, source_target_pairs={{1,0},{2,1},{3,2},{4,3},{5,4},{6,5},{7,6},{0,7},{9,8},{10,9},{11,1... | collective-permute-start | bytes 1548296 | tf_op jit(solution)/shard_map/ppermute | solution.py:25
  30.7 17.1 %collective-permute-done.1 = bf16[2,144,896]{2,1,0:T(8,128)(2,1)S(1)} collective-permute-done((bf16[2,144,896]{2,1,0:T(8,128)(2,1)S(1)}, bf16[2,144,896]{2,1,0:T(8,128)(2,1)S(1)}, u32[]{:S(2)}, u32[]{:S(2)}) %collective-permute-start.1) | collective-permute-done | bytes 516128 | tf_op jit(solution)/shard_map/ppermute | solution.py:23
  47.7 2.5 collective-permute-start.2
  50.2 12.2 %collective-permute-start.5 = (bf16[2,144,896]{2,1,0:T(8,128)(2,1)S(1)}, bf16[2,144,896]{2,1,0:T(8,128)(2,1)S(1)}, u32[]{:S(2)}, u32[]{:S(2)}) collective-permute-start(bf16[2,144,896]{2,1,0:T(8,128)(2,1)S(1)} %collective-permute-done.4), channel_id=1, source_target_pairs={{1,0},{2,1},{3,2},{4,3},{5,4},{6,5},{7,6},{0,7},{9,8},{10,9},{11,1... | collective-permute-start | bytes 1548296 | tf_op jit(solution)/shard_map/ppermute | solution.py:25
  62.4 8.9 %collective-permute-done.2 = bf16[2,144,896]{2,1,0:T(8,128)(2,1)S(1)} collective-permute-done((bf16[2,144,896]{2,1,0:T(8,128)(2,1)S(1)}, bf16[2,144,896]{2,1,0:T(8,128)(2,1)S(1)}, u32[]{:S(2)}, u32[]{:S(2)}) %collective-permute-start.2) | collective-permute-done | bytes 516128 | tf_op jit(solution)/shard_map/ppermute | solution.py:23
  71.2 2.5 collective-permute-start.3
  73.7 0.8 mul.39
  74.5 0.0 collective-permute-done.5
  74.5 12.6 %collective-permute-start.6 = (bf16[2,144,896]{2,1,0:T(8,128)(2,1)S(1)}, bf16[2,144,896]{2,1,0:T(8,128)(2,1)S(1)}, u32[]{:S(2)}, u32[]{:S(2)}) collective-permute-start(bf16[2,144,896]{2,1,0:T(8,128)(2,1)S(1)} %collective-permute-done.5), channel_id=1, source_target_pairs={{1,0},{2,1},{3,2},{4,3},{5,4},{6,5},{7,6},{0,7},{9,8},{10,9},{11,1... | collective-permute-start | bytes 1548296 | tf_op jit(solution)/shard_map/ppermute | solution.py:25
  87.1 7.8 %collective-permute-done.3 = bf16[2,144,896]{2,1,0:T(8,128)(2,1)} collective-permute-done((bf16[2,144,896]{2,1,0:T(8,128)(2,1)S(1)}, bf16[2,144,896]{2,1,0:T(8,128)(2,1)}, u32[]{:S(2)}, u32[]{:S(2)}) %collective-permute-start.3) | collective-permute-done | bytes 516128 | tf_op jit(solution)/shard_map/ppermute | solution.py:23
  94.9 1.9 bitcast_dynamic-update-slice_fusion.7
  96.8 0.8 bitcast_dynamic-update-slice_fusion.6
  97.6 0.8 bitcast_dynamic-update-slice_fusion.5
  98.5 0.9 bitcast_dynamic-update-slice_fusion.4
  99.3 0.8 bitcast_dynamic-update-slice_fusion.3
  100.2 0.8 bitcast_dynamic-update-slice_fusion.2
  101.0 0.8 bitcast_dynamic-update-slice_fusion.1
  101.9 0.0 collective-permute-done.6
  101.9 0.8 bitcast_dynamic-update-slice_fusion
  102.7 5.1 %gather_fusion = bf16[8,2,144,896]{3,2,1,0:T(8,128)(2,1)} fusion(bf16[8,2,144,896]{3,2,1,0:T(8,128)(2,1)} %bitcast_dynamic-update-slice_fusion, s32[1024]{0:T(1024)S(1)} %pad_clamp_fusion), kind=kCustom, calls=%fused_computation | custom fusion | bytes 8257568 | tf_op jit(solution)/shard_map/gather | solution.py:28
  107.8 3.5 %copy.27 = bf16[2,144,8,896]{3,2,1,0:T(8,128)(2,1)S(1)} copy(bf16[2,144,8,896]{3,1,0,2:T(8,128)(2,1)} %bitcast.51) | data formatting | bytes 8257536 | tf_op jit(solution)/shard_map/transpose | solution.py:8
  111.4 2.8 copy.36
  114.2 0.3 copy-done
  114.5 1.2 multiply_reduce_fusion
  115.7 0.1 mul.44
  115.8 0.0 copy-start.5
  115.8 6.6 %fusion.4 = f32[512,288]{0,1:T(8,128)S(1)} fusion(bf16[288,7168]{1,0:T(8,128)(2,1)} %bitcast.55, bf16[512,7168]{1,0:T(8,128)(2,1)} %all-gather.2.cloned.1.call-done, f32[7168]{0:T(1024)S(1)} %copy-done.2, f32[288]{0:T(512)S(1)} %mul.44), kind=kOutput, calls=%fused_computation.7 | convolution fusion | flops 2125086720 | bytes 12088448 | tf_op jit(solution)/shard_map/dot_general | solution.py:32
  122.4 1.3 copy.28
  123.7 3.5 %all-to-all-start = ((f32[512,2,144]{2,1,0:T(2,128)}), f32[512,2,144]{2,1,0:T(2,128)S(1)}, u32[]{:S(2)}, u32[]{:S(2)}) async-start(f32[512,2,144]{2,1,0:T(2,128)} %copy.28), calls=%async_computation | async-start | bytes 2097152 | tf_op jit(solution)/shard_map/all_to_all | solution.py:64
  127.2 0.0 reduce-scatter.2.cloned.1.call-start
  127.3 0.1 add.55
  127.4 0.1 copy.32
  127.5 14.1 %all-to-all-done = f32[512,2,144]{2,1,0:T(2,128)S(1)} async-done(((f32[512,2,144]{2,1,0:T(2,128)}), f32[512,2,144]{2,1,0:T(2,128)S(1)}, u32[]{:S(2)}, u32[]{:S(2)}) %all-to-all-start) | async-done | bytes 589856 | tf_op jit(solution)/shard_map/all_to_all | solution.py:64
  141.6 1.0 copy.34
  142.6 0.4 fusion.9
  143.0 0.4 exponential_reduce_fusion
  143.5 0.2 fusion.8
  143.7 8.7 %all_to_all.36 = bf16[128,8,144]{0,2,1:T(8,128)(2,1)S(1)} all-to-all(bf16[128,8,144]{0,2,1:T(8,128)(2,1)S(1)} %fusion.8), channel_id=1, replica_groups=mesh['cls'=4,'prt'=8] {'cls'}, dimensions={1} | all-to-all | bytes 589824 | tf_op jit(solution)/shard_map/all_to_all | solution.py:66
  152.4 8.6 %fusion.1 = f32[2,144,7168]{2,1,0:T(8,128)} fusion(bf16[512,7168]{1,0:T(8,128)(2,1)} %all-gather.2.cloned.1.call-done, bf16[4,2,18,8,128]{4,3,2,1,0:T(8,128)(2,1)S(1)} %bitcast.56), kind=kOutput, calls=%fused_computation.4 | convolution fusion | flops 2113929216 | bytes 15892480 | tf_op jit(solution)/shard_map/ijr,if->jrf/dot_general | solution.py:67
  161.0 0.0 reduce-scatter.2.cloned.1.call-update
  161.0 0.2 convert_reduce_fusion
  161.1 21.0 %psum.7 = f32[2,144]{1,0:T(2,128)} all-reduce(f32[2,144]{1,0:T(2,128)S(1)} %convert_reduce_fusion), channel_id=1, replica_groups=mesh['cls'=4,'prt'=8] {'prt'}, use_global_device_ids=true, to_apply=%region_6.7 | all-reduce | flops 288 | bytes 2304 | tf_op jit(solution)/shard_map/psum | solution.py:70
  182.2 123.2 %reduce-scatter.2.cloned.1.call-done = f32[2,144,896]{2,1,0:T(8,128)} async-done(((f32[2,144,7168]{2,1,0:T(8,128)}), f32[2,144,896]{2,1,0:T(8,128)}) %reduce-scatter.2.cloned.1.call-update) | async-done | bytes 1032208 | tf_op jit(solution)/shard_map/reduce_scatter | solution.py:69
  (21 shorter events, 0.1 us)
Async XLA Ops:
  7.2 92.2 %copy-start.1 = (bf16[2,144,896]{2,1,0:T(8,128)(2,1)S(1)}, bf16[2,144,896]{2,1,0:T(8,128)(2,1)}, u32[]{:S(2)}) copy-start(bf16[2,144,896]{2,1,0:T(8,128)(2,1)} %param.6) | copy-start | bytes 1548292
  7.2 108.6 %all-gather.2.cloned.1.call-start = ((), (), s32[]{:S(2)}) async-start(), calls=%async_computation.3 | async-start | bytes 9175040 | tf_op jit(solution)/shard_map/all_gather | solution.py:61
  7.9 18.0 %collective-permute-start = (bf16[2,144,896]{2,1,0:T(8,128)(2,1)}, bf16[2,144,896]{2,1,0:T(8,128)(2,1)S(1)}, u32[]{:S(2)}, u32[]{:S(2)}) collective-permute-start(bf16[2,144,896]{2,1,0:T(8,128)(2,1)} %param.6), channel_id=1, source_target_pairs={{0,1},{1,2},{2,3},{3,4},{4,5},{5,6},{6,7},{7,0},{8,9},{9,10},{10,1... | collective-permute-start | bytes 1548296 | tf_op jit(solution)/shard_map/ppermute | solution.py:23
  26.0 21.8 %collective-permute-start.1 = (bf16[2,144,896]{2,1,0:T(8,128)(2,1)S(1)}, bf16[2,144,896]{2,1,0:T(8,128)(2,1)S(1)}, u32[]{:S(2)}, u32[]{:S(2)}) collective-permute-start(bf16[2,144,896]{2,1,0:T(8,128)(2,1)S(1)} %collective-permute-done), channel_id=1, source_target_pairs={{0,1},{1,2},{2,3},{3,4},{4,5},{5,6},{6,7},{7,0},{8,9},{9,10},{10,1... | collective-permute-start | bytes 1548296 | tf_op jit(solution)/shard_map/ppermute | solution.py:23
  26.0 24.3 %collective-permute-start.4 = (bf16[2,144,896]{2,1,0:T(8,128)(2,1)}, bf16[2,144,896]{2,1,0:T(8,128)(2,1)S(1)}, u32[]{:S(2)}, u32[]{:S(2)}) collective-permute-start(bf16[2,144,896]{2,1,0:T(8,128)(2,1)} %param.6), channel_id=1, source_target_pairs={{1,0},{2,1},{3,2},{4,3},{5,4},{6,5},{7,6},{0,7},{9,8},{10,9},{11,1... | collective-permute-start | bytes 1548296 | tf_op jit(solution)/shard_map/ppermute | solution.py:25
  47.7 23.5 %collective-permute-start.2 = (bf16[2,144,896]{2,1,0:T(8,128)(2,1)S(1)}, bf16[2,144,896]{2,1,0:T(8,128)(2,1)S(1)}, u32[]{:S(2)}, u32[]{:S(2)}) collective-permute-start(bf16[2,144,896]{2,1,0:T(8,128)(2,1)S(1)} %collective-permute-done.1), channel_id=1, source_target_pairs={{0,1},{1,2},{2,3},{3,4},{4,5},{5,6},{6,7},{7,0},{8,9},{9,10},{10,1... | collective-permute-start | bytes 1548296 | tf_op jit(solution)/shard_map/ppermute | solution.py:23
  50.2 24.3 %collective-permute-start.5 = (bf16[2,144,896]{2,1,0:T(8,128)(2,1)S(1)}, bf16[2,144,896]{2,1,0:T(8,128)(2,1)S(1)}, u32[]{:S(2)}, u32[]{:S(2)}) collective-permute-start(bf16[2,144,896]{2,1,0:T(8,128)(2,1)S(1)} %collective-permute-done.4), channel_id=1, source_target_pairs={{1,0},{2,1},{3,2},{4,3},{5,4},{6,5},{7,6},{0,7},{9,8},{10,9},{11,1... | collective-permute-start | bytes 1548296 | tf_op jit(solution)/shard_map/ppermute | solution.py:25
  71.2 23.7 %collective-permute-start.3 = (bf16[2,144,896]{2,1,0:T(8,128)(2,1)S(1)}, bf16[2,144,896]{2,1,0:T(8,128)(2,1)}, u32[]{:S(2)}, u32[]{:S(2)}) collective-permute-start(bf16[2,144,896]{2,1,0:T(8,128)(2,1)S(1)} %collective-permute-done.2), channel_id=1, source_target_pairs={{0,1},{1,2},{2,3},{3,4},{4,5},{5,6},{6,7},{7,0},{8,9},{9,10},{10,1... | collective-permute-start | bytes 1548296 | tf_op jit(solution)/shard_map/ppermute | solution.py:23
  74.5 27.4 %collective-permute-start.6 = (bf16[2,144,896]{2,1,0:T(8,128)(2,1)S(1)}, bf16[2,144,896]{2,1,0:T(8,128)(2,1)S(1)}, u32[]{:S(2)}, u32[]{:S(2)}) collective-permute-start(bf16[2,144,896]{2,1,0:T(8,128)(2,1)S(1)} %collective-permute-done.5), channel_id=1, source_target_pairs={{1,0},{2,1},{3,2},{4,3},{5,4},{6,5},{7,6},{0,7},{9,8},{10,9},{11,1... | collective-permute-start | bytes 1548296 | tf_op jit(solution)/shard_map/ppermute | solution.py:25
  111.4 3.1 copy-start
  114.5 1.3 copy-start.2
  115.8 11.5 %copy-start.3 = (s32[128,2]{0,1:T(2,128)S(1)}, s32[128,2]{0,1:T(2,128)}, u32[]{:S(2)}) copy-start(s32[128,2]{0,1:T(2,128)} %param.9) | copy-start | bytes 3076
  115.8 11.5 %copy-start.5 = (f32[8]{0:T(128)S(1)}, f32[8]{0:T(128)}, u32[]{:S(2)}) copy-start(f32[8]{0:T(128)} %param.8) | copy-start | bytes 100
  123.7 17.9 %all-to-all-start = ((f32[512,2,144]{2,1,0:T(2,128)}), f32[512,2,144]{2,1,0:T(2,128)S(1)}, u32[]{:S(2)}, u32[]{:S(2)}) async-start(f32[512,2,144]{2,1,0:T(2,128)} %copy.28), calls=%async_computation | async-start | bytes 2097152 | tf_op jit(solution)/shard_map/all_to_all | solution.py:64
  127.2 178.1 %reduce-scatter.2.cloned.1.call-start = ((), (), s32[]{:S(2)}) async-start(), calls=%async_computation.4 | async-start | bytes 9289728 | tf_op jit(solution)/shard_map/reduce_scatter | solution.py:69
  143.4 17.5 %copy-start.4 = (f32[128]{0:T(128)}, f32[128]{0:T(128)S(1)}, u32[]{:S(2)}) copy-start(f32[128]{0:T(128)S(1)} %log_add_fusion) | copy-start | bytes 1540
Sparse Core Ops, SparseCore 0:
  9.5 55.0 all-gather.1
  161.1 144.1 reduce-scatter.1
